TPU v7x, 32 devices: a whole 2x2x4 slice. The times are simulated.
32 devices in a mesh: groups: 2 (over y), pairs: 4 (over z), section: 2 (over core), sub: 2 (over x).
Axes of the slice: x: 2, y: 2, z: 4, core: 2. Of those that a mesh axis runs over, the one named last changes fastest.
Arguments:
- raw_record: bfloat16 [64, 49152], P(('groups', 'pairs', 'section'), 'sub'), parts along dimension 0, may hold values from -6 to 6
- fir_taps: float32 [64], replicated, may hold values from -0.75 to 0.75
- channel_ids: int32 [64], P('groups'), parts along dimension 0, may hold values from 0 to 31, each once
- offsets: int32 [8], P(('groups', 'sub')), parts along dimension 0, may hold values from 0 to 16324
- pair_table: int32 [32, 2], P('groups'), parts along dimension 0, may hold values from -1 to 3, as said below
Outputs:
- correlations: float32 [8, 32, 8, 2048], P(('section', 'sub'), ('groups', 'pairs')), parts along dimension 1
There are 2 independent parts, one for each index of `groups`. A program takes and returns all parts, laid end to end along the dimension named above; an argument that names none is the same for every part. Nothing has to cross between parts.
Inputs may be any that keep to these rules, and one draw needn't show every extreme that they name: `pair_table`: each row is a pair block (I, J) with I <= J, or (-1, -1) for an empty slot. Every pair block of the 4 x 4 triangle stands in exactly one slot; all live slots of one owner share the first block I; owners p and p + 2 together hold exactly 5 pair blocks; some owner fills all 4 slots.
All inputs are finite; a program needn't handle non-finite values.
Results may differ from a plain program's by a relative error of at most 0.0075.
Values may be sent and summed in bfloat16 or wider, within the bound.
A program may use at most 128 MiB of HBM per device.

v0:
```python
import functools
import math

import jax
import jax.numpy as jnp
import numpy as np
from jax import lax
from jax.experimental import pallas as pl
from jax.experimental.pallas import tpu as pltpu
from jax.sharding import PartitionSpec as P

NF = 2048
TAPS = 64
DEC = 4
BAND = 64
LANES = 128
FINE = LANES // DEC
COARSE = NF // FINE
BANDS = NF // 2 // BAND
REACH = 3
MESH = pl.DeviceIdType.MESH


def round_bf16(values):
    return np.asarray(values).astype(jnp.bfloat16)


@functools.cache
def tables():
    n2 = np.arange(COARSE)[:, None]
    k2 = np.arange(BAND)[None, :]
    angle = 2 * np.pi * (n2 * k2 % COARSE) / COARSE
    c, s = np.cos(angle), np.sin(angle)
    dft = np.concatenate([c, -s, -s, -c], axis=1)
    high = round_bf16(dft)
    low = round_bf16(dft - high.astype(np.float64))
    forward = np.concatenate([high, low], axis=0)
    n1 = np.arange(FINE)[:, None]
    turn = 2 * np.pi * (n1 * k2) / NF
    turn = np.concatenate([turn, turn], axis=1)
    twiddle = np.stack([np.cos(turn), np.sin(turn)]).astype(np.float32)
    bins = np.arange(NF // 2)[:, None]
    lag = (np.arange(NF)[None, :] + NF // 2) % NF
    theta = 2 * np.pi * (bins * lag % NF) / NF
    weight = np.where(bins == 0, 1.0, 2.0) / math.sqrt(NF)
    re = (weight * np.cos(theta)).reshape(BANDS, BAND, NF)
    im = (-weight * np.sin(theta)).reshape(BANDS, BAND, NF)
    inverse = round_bf16(np.concatenate([re, im], axis=1).reshape(NF, NF))
    return forward, twiddle, inverse


def turned(pair, index, size):
    y, ys = pair
    index = index % size
    if index == 0:
        return y, ys
    if index * 4 == size:
        return ys, -y
    c = math.cos(2 * math.pi * index / size)
    s = math.sin(2 * math.pi * index / size)
    return c * y + s * ys, c * ys - s * y


def fft(pairs):
    size = len(pairs)
    if size == 1:
        return pairs
    even, odd = fft(pairs[0::2]), fft(pairs[1::2])
    low, high = [], []
    for k in range(size // 2):
        a, b = even[k], turned(odd[k], k, size)
        low.append((a[0] + b[0], a[1] + b[1]))
        high.append((a[0] - b[0], a[1] - b[1]))
    return low + high


def kernel(sizes, raw_in, taps_in, ids_in, offs_in, table_in, forward_in, twiddle_in, inverse, out,
           raw, taps, ids, offs, table, forward, twiddle, in_sems,
           held, rawf, tapf, zbuf, lhs, inv, inv_sem, z_send, x_send, c_send, recv):
    pairs, subs, rows, wins, slots, leads = sizes
    unit = rows * wins
    block = 2 * rows
    p = lax.axis_index("pairs")
    sec = lax.axis_index("section")
    sub = lax.axis_index("sub")

    barrier = pltpu.get_barrier_semaphore()
    for dp in range(pairs):
        for d in range(subs):
            if dp or d:
                pl.semaphore_signal(
                    barrier, inc=1, device_id_type=MESH,
                    device_id={"pairs": lax.rem(p + dp, pairs), "sub": lax.rem(sub + d, subs)})
    pl.semaphore_signal(barrier, inc=1, device_id={"section": 1 - sec}, device_id_type=MESH)

    loads = [
        pltpu.make_async_copy(source, target, in_sems.at[i])
        for i, (source, target) in enumerate(
            ((taps_in, taps), (offs_in, offs), (raw_in, raw), (forward_in, forward),
             (twiddle_in, twiddle), (ids_in, ids), (table_in, table)))
    ]
    for load in loads:
        load.start()
    load_inverse = pltpu.make_async_copy(inverse, inv, inv_sem)
    load_inverse.start()
    tapf[...] = jnp.zeros_like(tapf)
    for load in loads:
        load.wait()

    chunks = raw.shape[1] // LANES
    for m in range(chunks):
        rawf[m * 8 : m * 8 + rows, :] = raw[:, m * LANES : (m + 1) * LANES].astype(jnp.float32)
    rawf[chunks * 8 :, :] = jnp.zeros((rawf.shape[0] - chunks * 8, LANES), jnp.float32)
    tapf[0:1, 0:TAPS] = taps[...]

    wide = REACH * LANES
    tap_rows = jnp.broadcast_to(tapf[0:1, :], (FINE, wide))
    step = DEC * lax.broadcasted_iota(jnp.int32, (FINE, wide), 0)
    for w in range(wins):
        off = offs[w]
        first, rest = off // LANES, off % LANES
        shift = step + rest
        x = tap_rows
        for b in range((LANES + DEC * FINE - 1).bit_length()):
            x = jnp.where((shift >> b) & 1 == 1, pltpu.roll(x, 1 << b, 1), x)
        high = x.astype(jnp.bfloat16)
        low = (x - high.astype(jnp.float32)).astype(jnp.bfloat16)
        toeplitz = jnp.concatenate([high, low], axis=0)
        total = jnp.zeros((2 * FINE, rows * COARSE), jnp.float32)
        for s in range(REACH):
            seen = jnp.concatenate(
                [rawf[pl.ds((first + s) * 8 + r, COARSE, stride=8), :] for r in range(rows)], axis=0
            ).astype(jnp.bfloat16)
            total = total + lax.dot_general(
                toeplitz[:, s * LANES : (s + 1) * LANES], seen, (((1,), (1,)), ((), ())),
                preferred_element_type=jnp.float32)
        deci = (total[:FINE] + total[FINE:]).astype(jnp.bfloat16)
        for r in range(rows):
            part = deci[:, r * COARSE : (r + 1) * COARSE]
            z = jnp.dot(part, forward[:COARSE, :], preferred_element_type=jnp.float32) + jnp.dot(
                part, forward[COARSE:, :], preferred_element_type=jnp.float32)
            at = (w * rows + r) * FINE
            zbuf[0, at : at + FINE, :] = z[:, :LANES]
            zbuf[1, at : at + FINE, :] = z[:, LANES:]
    points = []
    for n in range(FINE):
        y = zbuf[0, pl.ds(n, unit, stride=FINE), :]
        ys = zbuf[1, pl.ds(n, unit, stride=FINE), :]
        c, s = twiddle[0, n : n + 1, :], twiddle[1, n : n + 1, :]
        points.append((c * y + s * ys, c * ys - s * y))
    bins = fft(points)
    mine = (p * 2 + sec) * subs + sub
    for k in range(BANDS):
        x = bins[k][0]
        power = jnp.sum(x * x, axis=1, keepdims=True) * (1.0 / BAND)
        held[mine, :, k * LANES : (k + 1) * LANES] = (x * lax.rsqrt(power + 1e-06)).astype(jnp.bfloat16)

    pl.semaphore_wait(barrier, pairs * subs)

    def send(slot, send_sem, device):
        return pltpu.make_async_remote_copy(
            src_ref=held.at[slot], dst_ref=held.at[slot], send_sem=send_sem,
            recv_sem=recv.at[slot], device_id=device, device_id_type=MESH)

    near = [p]
    for i in range(1, pairs):
        at = jnp.int32(0)
        for q in range(pairs):
            at = jnp.where(p == q, sorted(range(pairs), key=lambda t: (abs(t - q), t))[i], at)
        near.append(at)
    copies = []
    for dp in range(pairs - 1, -1, -1):
        for d in range(subs - 1, -1, -1):
            if not (dp or d):
                continue
            copies.append(send(mine, x_send.at[dp, d], {"pairs": near[dp], "sub": lax.rem(sub + d, subs)}))
            copies[-1].start()
    for dp in range(pairs):
        slot = (near[dp] * 2 + sec) * subs + sub
        if dp:
            send(slot, z_send.at[0], {"section": 1 - sec}).wait_recv()
        copies.append(send(slot, c_send.at[dp, 0], {"section": 1 - sec}))
        copies[-1].start()
    for dp in range(pairs):
        for d in range(1, subs):
            slot = (near[dp] * 2 + sec) * subs + lax.rem(sub + d, subs)
            send(slot, z_send.at[0], {"section": 1 - sec}).wait_recv()
            copies.append(send(slot, c_send.at[dp, d], {"section": 1 - sec}))
            copies[-1].start()

    count = pairs * block
    lead_rows = leads * subs * unit
    depth = pairs * 2 * subs * unit
    col = lax.broadcasted_iota(jnp.int32, (1, depth), 1)
    col_row = (col // (unit * subs)) * rows + col % rows
    plain = lax.broadcasted_iota(jnp.int32, (1, count), 1)
    col_id = jnp.full((1, depth), -1, jnp.int32)
    row_id = jnp.full((1, count), -1, jnp.int32)
    for i in range(count):
        col_id = jnp.where(col_row == i, ids[i], col_id)
        row_id = jnp.where(plain == i, ids[i], row_id)
    line = lax.broadcasted_iota(jnp.int32, (lead_rows, 1), 0)
    own = table[0, p * slots]
    for s in range(1, slots):
        own = jnp.maximum(own, table[0, p * slots + s])
    lead = own * block + (sec * subs + sub) * leads + line // (subs * unit)
    place = (line // rows) % (subs * wins)
    col_place = (col // unit) % subs * wins + (col // rows) % wins
    pick = jnp.where((lead == col_id) & (place == col_place), 1.0, 0.0).astype(jnp.bfloat16)
    entry = lax.broadcasted_iota(jnp.int32, (slots * block, 1), 0)
    want = jnp.full((slots * block, 1), -1, jnp.int32)
    for s in range(slots):
        live = jnp.where(table[0, p * slots + s] >= 0, table[1, p * slots + s] * block, -block)
        want = jnp.where(entry // block == s, live + entry % block, want)
    order = jnp.where(want == row_id, 1.0, 0.0).astype(jnp.bfloat16)

    for dp in range(pairs):
        for d in range(subs):
            slot = (lax.rem(p + dp, pairs) * 2 + 1 - sec) * subs + lax.rem(sub + d, subs)
            send(slot, z_send.at[0], {"section": 1 - sec}).wait_recv()
    for copy in copies:
        copy.wait_send()

    left = lax.broadcasted_iota(jnp.int32, (8, LANES), 1) < BAND
    top = lax.broadcasted_iota(jnp.int32, (8, LANES), 0) < rows
    scale = 1.0 / (wins * subs)
    width = 2 * LANES

    for base in range(0, NF, width):
        every = held[:, :, pl.ds(base, width)].astype(jnp.float32)
        flat = every.reshape(depth, width)
        heads = jnp.dot(pick, flat.astype(jnp.bfloat16), preferred_element_type=jnp.float32)
        crossed = [[[] for _ in range(2)] for _ in range(leads)]
        for h in range(2):
            lanes = slice(h * LANES, (h + 1) * LANES)
            half = heads[:, lanes]
            swap = pltpu.roll(half, BAND, 1)
            for q in range(pairs):
                for a in range(leads):
                    sums = []
                    for source in (half, swap):
                        two = []
                        for c in range(2):
                            t = None
                            for u in range(subs):
                                g = (q * 2 + c) * subs + u
                                at = (a * subs + u) * unit
                                v = flat[g * unit : (g + 1) * unit, lanes] * source[at : at + unit, :]
                                t = v if t is None else t + v
                            two.append(t + pltpu.roll(t, rows, 0))
                        sums.append(jnp.where(top, two[0], two[1]))
                    re, im = sums
                    crossed[a][h].append(
                        jnp.where(left, re + pltpu.roll(re, BAND, 1), pltpu.roll(im, BAND, 1) - im) * scale)
        for a in range(leads):
            cross = jnp.concatenate(
                [jnp.concatenate(crossed[a][h], axis=0) for h in range(2)], axis=1).astype(jnp.bfloat16)
            got = jnp.dot(order, cross, preferred_element_type=jnp.float32)
            lhs[a * slots * block : (a + 1) * slots * block, pl.ds(base, width)] = got.astype(jnp.bfloat16)

    load_inverse.wait()

    for base in range(0, NF, width):
        out[:, pl.ds(base, width)] = jnp.dot(
            lhs[...], inv[:, pl.ds(base, width)], preferred_element_type=jnp.float32)


def solution(mesh):
    pairs, subs = mesh.shape["pairs"], mesh.shape["sub"]

    def body(raw_record, fir_taps, channel_ids, offsets, pair_table):
        rows, wins = raw_record.shape[0], offsets.shape[0]
        slots = pair_table.shape[0] // pairs
        block = 2 * rows
        leads = block // (2 * subs)
        unit = rows * wins
        assert unit == 8 and block == 8 and wins == 2
        chunks = raw_record.shape[1] // LANES
        units = pairs * 2 * subs
        vmem = pl.BlockSpec(memory_space=pltpu.VMEM)
        hbm = pl.BlockSpec(memory_space=pltpu.HBM)
        forward, twiddle, inverse = tables()
        total = leads * slots * block
        result = pl.pallas_call(
            functools.partial(kernel, (pairs, subs, rows, wins, slots, leads)),
            out_shape=jax.ShapeDtypeStruct((total, NF), jnp.float32),
            in_specs=[hbm] * 8,
            out_specs=vmem,
            scratch_shapes=[
                pltpu.VMEM(raw_record.shape, raw_record.dtype),
                pltpu.VMEM((1, TAPS), jnp.float32),
                pltpu.SMEM(channel_ids.shape, jnp.int32),
                pltpu.SMEM(offsets.shape, jnp.int32),
                pltpu.SMEM(pair_table.shape[::-1], jnp.int32),
                pltpu.VMEM(forward.shape, jnp.bfloat16),
                pltpu.VMEM(twiddle.shape, jnp.float32),
                pltpu.SemaphoreType.DMA((7,)),
                pltpu.VMEM((units, unit, NF), jnp.bfloat16),
                pltpu.VMEM(((chunks + 8) * 8, LANES), jnp.float32),
                pltpu.VMEM((8, REACH * LANES), jnp.float32),
                pltpu.VMEM((2, unit * FINE, LANES), jnp.float32),
                pltpu.VMEM((total, NF), jnp.bfloat16),
                pltpu.VMEM((NF, NF), jnp.bfloat16),
                pltpu.SemaphoreType.DMA,
                pltpu.SemaphoreType.DMA((pairs,)),
                pltpu.SemaphoreType.DMA((pairs, subs)),
                pltpu.SemaphoreType.DMA((pairs, subs)),
                pltpu.SemaphoreType.DMA((units,)),
            ],
            compiler_params=pltpu.CompilerParams(
                collective_id=0, has_side_effects=True, vmem_limit_bytes=48*2**20),
        )(*[pltpu.with_memory_space_constraint(v, pltpu.HBM) for v in (raw_record, fir_taps.reshape(1, TAPS), channel_ids, offsets, pair_table.T,
          jnp.asarray(forward), jnp.asarray(twiddle), jnp.asarray(inverse))])
        return result.reshape(leads, slots, block, NF)

    return jax.shard_map(
        body,
        mesh=mesh,
        in_specs=(
            P(("groups", "pairs", "section"), "sub"),
            P(),
            P("groups"),
            P(("groups", "sub")),
            P("groups", None),
        ),
        out_specs=P(("section", "sub"), ("groups", "pairs"), None, None),
        check_vma=False,
    )
```

profile of v0, /device:TPU:1, one launch (start us, length us, event | category | flops | bytes accessed | tf_op | source)
XLA Modules:
  0.0 16.8 jit_solution(2837091550380183357)
XLA Ops:
  0.0 16.0 %shard_map.82 = f32[64,2048]{1,0:T(8,128)S(1)} custom-call(bf16[4,24576]{1,0:T(4,128)(2,1)} %raw_in.1, f32[1,64]{1,0:T(1,128)} %bitcast.5, s32[32]{0:T(128)} %ids_in.1, s32[2]{0:T(128)} %offs_in.1, s32[2,16]{1,0:T(2,128)} %bitcast.4, bf16[128,256]{1,0:T(8,128)(2,1)} %constant.6.clone.forward_in, f32[2,32,128]{2,1,0:T(8,128)} %constant.7.clone.twiddle_in, ...), custom_call_target="tpu_custom_call" | custom-call | tf_op jit(solution)/shard_map/pallas_call | solution.py:284
  16.0 0.8 %copy.10 = f32[2,4,8,2048]{3,2,1,0:T(8,128)} copy(f32[2,4,8,2048]{3,2,1,0:T(8,128)S(1)} %bitcast.3) | data formatting | bytes 1048576
where the time goes:
time: 17.1 us; the launch traced here: 16.8 us
  Pallas kernels  16 us (94%)
  local copies, waits for them, and re-layouts  0.8 us (5%)
    pallas_call x1, Pallas kernels, body(): pl.pallas_call(functools.partial(kernel, (pairs, subs, rows, wins, slots,...  16 us
    unnamed x1, local copies, waits for them, and re-layouts  0.8 us

commit v1 on v0

v1 whole, which is shorter than its diff:
```python
import functools
import math

import jax
import jax.numpy as jnp
import numpy as np
from jax import lax
from jax.experimental import pallas as pl
from jax.experimental.pallas import tpu as pltpu
from jax.sharding import PartitionSpec as P

NF = 2048
TAPS = 64
DEC = 4
BAND = 64
LANES = 128
RADIX = 8
HALF = 4
FINE = LANES // DEC
REACH = 3
SPREAD = REACH + DEC - 1
PIECES = DEC * (NF // LANES)
MESH = pl.DeviceIdType.MESH


def round_bf16(values):
    return np.asarray(values).astype(jnp.bfloat16)


@functools.cache
def tables():
    kappa = np.arange(LANES)
    angle = 2 * np.pi * (kappa[:, None] * kappa[None, :] % (2 * LANES)) / (2 * LANES)
    c, s = np.cos(angle), np.sin(angle)
    dft = np.block([[c, -s], [s, c]])
    high = round_bf16(dft)
    low = round_bf16(dft - high.astype(np.float64))
    forward = np.concatenate([high, low], axis=0)
    n1 = (np.arange(8) // HALF * LANES)[:, None] + kappa[None, :]
    turn = 2 * np.pi * np.arange(RADIX)[:, None, None] * n1[None] / NF
    twiddle = np.stack([np.cos(turn), np.sin(turn)], axis=1).astype(np.float32)
    weight = 2.0 / math.sqrt(NF)
    cols = []
    for h in range(2):
        j1 = h * LANES + kappa
        theta = 2 * np.pi * (kappa[:, None] * j1[None, :] % (2 * LANES)) / (2 * LANES)
        c, s = weight * np.cos(theta), weight * np.sin(theta)
        cols.append(np.block([[c, s], [-s, c]]))
    inverse = round_bf16(np.concatenate(cols, axis=1))
    turn = 2 * np.pi * np.arange(RADIX)[:, None] * np.arange(2 * LANES)[None, :] / NF
    back = np.concatenate([np.cos(turn), np.sin(turn)], axis=0).astype(np.float32)
    return forward, twiddle, inverse, back


def spread8(d):
    c = math.sqrt(0.5)
    a = [d[i] + d[i + 4] for i in range(4)]
    m = [d[i] - d[i + 4] for i in range(4)]
    even, odd = a[0] + a[2], a[1] + a[3]
    u, v = c * (m[1] - m[3]), c * (m[1] + m[3])
    y1 = (m[0] + u, -m[2] - v)
    y3 = (m[0] - u, m[2] - v)
    y2 = (a[0] - a[2], a[3] - a[1])
    back = [(r, -i) for r, i in (y3, y2, y1)]
    return [(even + odd, None), y1, y2, y3, (even - odd, None)] + back


def gather8(x):
    c = math.sqrt(0.5)
    e0, o0 = x[0][0] + x[4][0], x[0][0] - x[4][0]
    p = [x[b][0] + x[8 - b][0] for b in (1, 2, 3)]
    q = [x[8 - b][1] - x[b][1] for b in (1, 2, 3)]
    pp, pm = p[0] + p[2], c * (p[0] - p[2])
    qm, qp = q[0] - q[2], c * (q[0] + q[2])
    ep, em = e0 + p[1], e0 - p[1]
    op, om = o0 + q[1], o0 - q[1]
    f, g = pm + qp, pm - qp
    return [ep + pp, op + f, em + qm, om - g, ep - pp, op - f, em - qm, om + g]


def kernel(sizes, raw_in, taps_in, ids_in, offs_in, table_in, forward_in, twiddle_in, inverse_in, back_in, out,
           raw, taps, ids, offs, table, forward, twiddle, in_sems,
           held, tapf, shifted, lhs, inv, back, late_sems, z_send, x_send, c_send, recv):
    pairs, subs, rows, wins, slots, leads = sizes
    unit = rows * wins
    block = 2 * rows
    p = lax.axis_index("pairs")
    sec = lax.axis_index("section")
    sub = lax.axis_index("sub")

    barrier = pltpu.get_barrier_semaphore()
    for dp in range(pairs):
        for d in range(subs):
            if dp or d:
                pl.semaphore_signal(
                    barrier, inc=1, device_id_type=MESH,
                    device_id={"pairs": lax.rem(p + dp, pairs), "sub": lax.rem(sub + d, subs)})
    pl.semaphore_signal(barrier, inc=1, device_id={"section": 1 - sec}, device_id_type=MESH)

    loads = [
        pltpu.make_async_copy(source, target, in_sems.at[i])
        for i, (source, target) in enumerate(
            ((taps_in, taps), (offs_in, offs), (raw_in, raw.at[:, pl.ds(0, raw_in.shape[1])]), (forward_in, forward),
             (twiddle_in, twiddle), (ids_in, ids), (table_in, table)))
    ]
    for load in loads:
        load.start()
    late = [
        pltpu.make_async_copy(source, target, late_sems.at[i])
        for i, (source, target) in enumerate(((inverse_in, inv), (back_in, back)))
    ]
    for load in late:
        load.start()
    tapf[...] = jnp.zeros_like(tapf)
    span = raw_in.shape[1]
    raw[:, span:] = jnp.zeros((rows, raw.shape[1] - span), raw.dtype)
    seg = lax.broadcasted_iota(jnp.int32, (2 * LANES, LANES), 0) % LANES // RADIX
    same = seg == lax.broadcasted_iota(jnp.int32, (2 * LANES, LANES), 1) // RADIX
    mean = jnp.where(same, 1.0 / BAND, 0.0).astype(jnp.bfloat16)
    sign = 1.0 - 2.0 * (lax.broadcasted_iota(jnp.int32, (8, LANES), 1) % 2).astype(jnp.float32)
    line8 = lax.broadcasted_iota(jnp.int32, (8, LANES), 0)
    top = line8 < HALF
    lane = lax.broadcasted_iota(jnp.int32, (FINE, LANES), 1)
    step = DEC * lax.broadcasted_iota(jnp.int32, (FINE, LANES), 0)
    for load in loads:
        load.wait()
    tapf[0:1, 0:TAPS] = taps[...]
    moved = jnp.broadcast_to(tapf[0:1, :], (8, LANES))
    for b in range(3):
        moved = jnp.where((line8 >> b) & 1 == 1, pltpu.roll(moved, 1 << b, 1), moved)
    for i in range(LANES // 8):
        ahead = pltpu.roll(moved, 8 * i, 1) if i else moved
        shifted[8 * i : 8 * i + 8, :] = ahead
        shifted[LANES + 8 * i : LANES + 8 * i + 8, :] = ahead
    blank = jnp.zeros((FINE, LANES), jnp.bfloat16)

    turned = []
    for w in range(wins):
        off = offs[w]
        first, rest = off // LANES, off % LANES
        rolled = shifted[pl.ds(rest, FINE, stride=DEC), :]
        highs, lows = [], []
        for s in range(REACH):
            t = lane + s * LANES - step - rest
            x = jnp.where((t >= 0) & (t < TAPS), rolled, 0.0)
            highs.append(x.astype(jnp.bfloat16))
            lows.append((x - highs[-1].astype(jnp.float32)).astype(jnp.bfloat16))
        cols = []
        for s in range(SPREAD):
            cols.append(jnp.concatenate(
                [part[s - f] if 0 <= s - f < REACH else blank for part in (highs, lows) for f in range(DEC)], axis=0))
        toeplitz = jnp.concatenate(cols, axis=1)
        seen = raw[:, pl.ds(first * LANES, (PIECES + SPREAD - DEC) * LANES)].astype(jnp.float32)
        piece = [seen[:, m * LANES : (m + 1) * LANES] for m in range(PIECES + SPREAD - DEC)]
        pair = [jnp.concatenate([piece[m], piece[m + DEC]], axis=0) for m in range(len(piece) - DEC)]
        data = jnp.concatenate(
            [jnp.concatenate([pair[s + 2 * DEC * n] for n in range(RADIX)], axis=0).astype(jnp.bfloat16)
             for s in range(SPREAD)], axis=1)
        total = lax.dot_general(data, toeplitz, (((1,), (1,)), ((), ())), preferred_element_type=jnp.float32)
        deci = (total[:, :LANES] + total[:, LANES:]).astype(jnp.bfloat16).astype(jnp.float32)
        parts = spread8([deci[8 * n : 8 * n + 8] for n in range(RADIX)])
        for b in range(RADIX):
            re, im = parts[b]
            c, s = twiddle[b, 0], twiddle[b, 1]
            if b == 0:
                re, im = re, jnp.zeros_like(re)
            elif im is None:
                re, im = re * c, -re * s
            else:
                re, im = re * c + im * s, im * c - re * s
            turned.append(jnp.concatenate([re, im], axis=1))
    z = jnp.concatenate(turned, axis=0)
    high = z.astype(jnp.bfloat16)
    low = (z - high.astype(jnp.float32)).astype(jnp.bfloat16)
    count_z = z.shape[0]
    both = jnp.dot(jnp.concatenate([high, low], axis=0), forward[: 2 * LANES, :], preferred_element_type=jnp.float32)
    both = both[:count_z] + both[count_z:] + jnp.dot(
        high, forward[2 * LANES :, :], preferred_element_type=jnp.float32)
    spectra = []
    power = None
    for b in range(RADIX):
        for part in range(2):
            lanes = slice(part * LANES, (part + 1) * LANES)
            u0 = both[b * 8 : b * 8 + 8, lanes]
            u1 = both[(RADIX + b) * 8 : (RADIX + b) * 8 + 8, lanes]
            near = jnp.where(top, u0, pltpu.roll(u1, HALF, 0))
            far = jnp.where(top, pltpu.roll(u0, HALF, 0), u1)
            x = near + sign * far
            spectra.append(x)
            power = x * x if power is None else power + x * x
    high = power.astype(jnp.bfloat16)
    low = (power - high.astype(jnp.float32)).astype(jnp.bfloat16)
    band = jnp.dot(jnp.concatenate([high, low], axis=1), mean, preferred_element_type=jnp.float32)
    gain = lax.rsqrt(band + 1e-06)
    mine = (p * 2 + sec) * subs + sub
    for b in range(RADIX):
        held[mine, :, b * LANES : (b + 1) * LANES] = jnp.concatenate(
            [spectra[2 * b] * gain, spectra[2 * b + 1] * gain], axis=0).astype(jnp.bfloat16)

    pl.semaphore_wait(barrier, pairs * subs)

    def send(slot, send_sem, device):
        return pltpu.make_async_remote_copy(
            src_ref=held.at[slot], dst_ref=held.at[slot], send_sem=send_sem,
            recv_sem=recv.at[slot], device_id=device, device_id_type=MESH)

    near = [p]
    for i in range(1, pairs):
        at = jnp.int32(0)
        for q in range(pairs):
            at = jnp.where(p == q, sorted(range(pairs), key=lambda t: (abs(t - q), t))[i], at)
        near.append(at)
    copies = []
    for dp in range(pairs - 1, -1, -1):
        for d in range(subs - 1, -1, -1):
            if not (dp or d):
                continue
            copies.append(send(mine, x_send.at[dp, d], {"pairs": near[dp], "sub": lax.rem(sub + d, subs)}))
            copies[-1].start()
    for dp in range(pairs):
        slot = (near[dp] * 2 + sec) * subs + sub
        if dp:
            send(slot, z_send.at[0], {"section": 1 - sec}).wait_recv()
        copies.append(send(slot, c_send.at[dp, 0], {"section": 1 - sec}))
        copies[-1].start()
    for dp in range(pairs):
        for d in range(1, subs):
            slot = (near[dp] * 2 + sec) * subs + lax.rem(sub + d, subs)
            send(slot, z_send.at[0], {"section": 1 - sec}).wait_recv()
            copies.append(send(slot, c_send.at[dp, d], {"section": 1 - sec}))
            copies[-1].start()

    count = pairs * block
    tall = 2 * unit
    depth = pairs * 2 * subs * tall
    col = lax.broadcasted_iota(jnp.int32, (1, depth), 1)
    col_row = (col // (tall * subs)) * rows + col % rows
    col_id = jnp.full((1, depth), -1, jnp.int32)
    for i in range(count):
        col_id = jnp.where(col_row == i, ids[i], col_id)
    own = table[0, p * slots]
    for s in range(1, slots):
        own = jnp.maximum(own, table[0, p * slots + s])
    group = subs * tall
    line = lax.broadcasted_iota(jnp.int32, (2 * leads * group, 1), 0)
    lead = own * block + (sec * subs + sub) * leads + line // group % leads
    place = line // tall % subs * wins + line // rows % wins
    col_place = col // tall % subs * wins + col // rows % wins
    line_part, col_part = line // unit % 2, col // unit % 2
    crossing = line // (group * leads)
    chosen = (lead == col_id) & (place == col_place) & ((line_part + crossing) % 2 == col_part)
    value = jnp.where((crossing == 1) & (line_part == 1), -1.0, 1.0)
    pick = jnp.where(chosen, value, 0.0).astype(jnp.bfloat16)
    entry = lax.broadcasted_iota(jnp.int32, (slots * block, 1), 0)
    want = jnp.full((slots * block, 1), -1, jnp.int32)
    for s in range(slots):
        live = jnp.where(table[0, p * slots + s] >= 0, table[1, p * slots + s] * block, -block)
        want = jnp.where(entry // block == s, live + entry % block, want)
    order = jnp.where(want == col_id, 1.0 / (wins * subs), 0.0).astype(jnp.bfloat16)

    for dp in range(pairs):
        for d in range(subs):
            slot = (lax.rem(p + dp, pairs) * 2 + 1 - sec) * subs + lax.rem(sub + d, subs)
            send(slot, z_send.at[0], {"section": 1 - sec}).wait_recv()

    width = 2 * LANES
    wanted = slots * block
    edge = jnp.where(lax.broadcasted_iota(jnp.int32, (wanted, LANES), 1) == 0, 0.5, 1.0)
    for base in range(0, RADIX, 2):
        flat = held[:, :, base * LANES : (base + 2) * LANES].reshape(depth, width)
        heads = jnp.dot(pick, flat, preferred_element_type=jnp.float32).astype(jnp.bfloat16)
        for a in range(leads):
            for part in range(2):
                at = (part * leads + a) * group
                full = jnp.concatenate([heads[at : at + group, :]] * (pairs * 2), axis=0)
                got = jnp.dot(order, flat * full, preferred_element_type=jnp.float32)
                for h in range(2):
                    x = got[:, h * LANES : (h + 1) * LANES]
                    if base + h == 0:
                        x = x * edge
                    lhs[base + h, a * wanted : (a + 1) * wanted, part * LANES : (part + 1) * LANES] = x.astype(jnp.bfloat16)

    for load in late:
        load.wait()

    for h in range(2):
        for a in range(leads):
            x = lhs[:, a * wanted : (a + 1) * wanted, :].reshape(RADIX * wanted, width)
            y = jnp.dot(x, inv[:, h * width : (h + 1) * width], preferred_element_type=jnp.float32)
            for g in range(wanted // 8):
                points = []
                for b in range(RADIX):
                    at = b * wanted + g * 8
                    re, im = y[at : at + 8, :LANES], y[at : at + 8, LANES:]
                    c = back[b : b + 1, h * LANES : (h + 1) * LANES]
                    s = back[RADIX + b : RADIX + b + 1, h * LANES : (h + 1) * LANES]
                    if b == 0:
                        points.append((re, None))
                    elif b == RADIX // 2:
                        points.append((re * c - im * s, None))
                    else:
                        points.append((re * c - im * s, re * s + im * c))
                lags = gather8(points)
                for j in range(RADIX):
                    column = (j + RADIX // 2) % RADIX * width + h * LANES
                    out[a * wanted + g * 8 : a * wanted + g * 8 + 8, column : column + LANES] = lags[j]

    for copy in copies:
        copy.wait_send()


def solution(mesh):
    pairs, subs = mesh.shape["pairs"], mesh.shape["sub"]

    def body(raw_record, fir_taps, channel_ids, offsets, pair_table):
        rows, wins = raw_record.shape[0], offsets.shape[0]
        slots = pair_table.shape[0] // pairs
        block = 2 * rows
        leads = block // (2 * subs)
        unit = rows * wins
        assert unit == 8 and block == 8 and wins == 2
        assert rows == HALF
        units = pairs * 2 * subs
        vmem = pl.BlockSpec(memory_space=pltpu.VMEM)
        hbm = pl.BlockSpec(memory_space=pltpu.HBM)
        forward, twiddle, inverse, back = tables()
        total = leads * slots * block
        result = pl.pallas_call(
            functools.partial(kernel, (pairs, subs, rows, wins, slots, leads)),
            out_shape=jax.ShapeDtypeStruct((total, NF), jnp.float32),
            in_specs=[hbm] * 9,
            out_specs=vmem,
            scratch_shapes=[
                pltpu.VMEM((rows, raw_record.shape[1] + LANES), raw_record.dtype),
                pltpu.VMEM((1, TAPS), jnp.float32),
                pltpu.SMEM(channel_ids.shape, jnp.int32),
                pltpu.SMEM(offsets.shape, jnp.int32),
                pltpu.SMEM(pair_table.shape[::-1], jnp.int32),
                pltpu.VMEM(forward.shape, jnp.bfloat16),
                pltpu.VMEM(twiddle.shape, jnp.float32),
                pltpu.SemaphoreType.DMA((7,)),
                pltpu.VMEM((units, 2 * unit, NF // 2), jnp.bfloat16),
                pltpu.VMEM((8, LANES), jnp.float32),
                pltpu.VMEM((2 * LANES, LANES), jnp.float32),
                pltpu.VMEM((RADIX, total, 2 * LANES), jnp.bfloat16),
                pltpu.VMEM(inverse.shape, jnp.bfloat16),
                pltpu.VMEM(back.shape, jnp.float32),
                pltpu.SemaphoreType.DMA((2,)),
                pltpu.SemaphoreType.DMA((pairs,)),
                pltpu.SemaphoreType.DMA((pairs, subs)),
                pltpu.SemaphoreType.DMA((pairs, subs)),
                pltpu.SemaphoreType.DMA((units,)),
            ],
            compiler_params=pltpu.CompilerParams(
                collective_id=0, has_side_effects=True, vmem_limit_bytes=48*2**20),
        )(*[pltpu.with_memory_space_constraint(v, pltpu.HBM) for v in (raw_record, fir_taps.reshape(1, TAPS), channel_ids, offsets, pair_table.T,
          jnp.asarray(forward), jnp.asarray(twiddle), jnp.asarray(inverse), jnp.asarray(back))])
        return result.reshape(leads, slots, block, NF)

    return jax.shard_map(
        body,
        mesh=mesh,
        in_specs=(
            P(("groups", "pairs", "section"), "sub"),
            P(),
            P("groups"),
            P(("groups", "sub")),
            P("groups", None),
        ),
        out_specs=P(("section", "sub"), ("groups", "pairs"), None, None),
        check_vma=False,
    )
```

time: 17.1 us -> 15.6 us (0.912)
  Pallas kernels: 16 us -> 14.7 us
    pallas_call x1, Pallas kernels: 16 us -> 14.7 us  [body(): pl.pallas_call(functools.partial(kernel, (pairs, subs, rows, wins, slots,...]
where the time goes in v1:
time: 15.6 us; the launch traced here: 15.5 us
  Pallas kernels  14.7 us (94%)
  local copies, waits for them, and re-layouts  0.8 us (5%)
    pallas_call x1, Pallas kernels, body(): pl.pallas_call(functools.partial(kernel, (pairs, subs, rows, wins, slots,...  14.7 us
    unnamed x1, local copies, waits for them, and re-layouts  0.8 us

profile of v1, /device:TPU:1, one launch (start us, length us, event | category | flops | bytes accessed | tf_op | source)
XLA Modules:
  0.0 15.5 jit_solution(7530727266318057349)
XLA Ops:
  0.0 14.7 %shard_map.91 = f32[64,2048]{1,0:T(8,128)S(1)} custom-call(bf16[4,24576]{1,0:T(4,128)(2,1)} %raw_in.1, f32[1,64]{1,0:T(1,128)} %bitcast.5, s32[32]{0:T(128)} %ids_in.1, s32[2]{0:T(128)} %offs_in.1, s32[2,16]{1,0:T(2,128)} %bitcast.4, bf16[512,256]{1,0:T(8,128)(2,1)} %constant.8.clone.forward_in, f32[8,2,8,128]{3,2,1,0:T(8,128)} %constant.9.clone.twiddle_in, ...), custom_call_target="tpu_custom_call" | custom-call | tf_op jit(solution)/shard_map/pallas_call | solution.py:328
  14.7 0.8 %copy.11 = f32[2,4,8,2048]{3,2,1,0:T(8,128)} copy(f32[2,4,8,2048]{3,2,1,0:T(8,128)S(1)} %bitcast.3) | data formatting | bytes 1048576

commit v2 on v1

--- a/solution.py
+++ b/solution.py
@@ -80,7 +80,7 @@
 
 def kernel(sizes, raw_in, taps_in, ids_in, offs_in, table_in, forward_in, twiddle_in, inverse_in, back_in, out,
            raw, taps, ids, offs, table, forward, twiddle, in_sems,
-           held, tapf, shifted, lhs, inv, back, late_sems, z_send, x_send, c_send, recv):
+           held, tapf, shifted, picks, orders, lhs, inv, back, late_sems, x_send, c_send, recv):
     pairs, subs, rows, wins, slots, leads = sizes
     unit = rows * wins
     block = 2 * rows
@@ -217,19 +217,6 @@
                 continue
             copies.append(send(mine, x_send.at[dp, d], {"pairs": near[dp], "sub": lax.rem(sub + d, subs)}))
             copies[-1].start()
-    for dp in range(pairs):
-        slot = (near[dp] * 2 + sec) * subs + sub
-        if dp:
-            send(slot, z_send.at[0], {"section": 1 - sec}).wait_recv()
-        copies.append(send(slot, c_send.at[dp, 0], {"section": 1 - sec}))
-        copies[-1].start()
-    for dp in range(pairs):
-        for d in range(1, subs):
-            slot = (near[dp] * 2 + sec) * subs + lax.rem(sub + d, subs)
-            send(slot, z_send.at[0], {"section": 1 - sec}).wait_recv()
-            copies.append(send(slot, c_send.at[dp, d], {"section": 1 - sec}))
-            copies[-1].start()
-
     count = pairs * block
     tall = 2 * unit
     depth = pairs * 2 * subs * tall
@@ -257,31 +244,40 @@
         live = jnp.where(table[0, p * slots + s] >= 0, table[1, p * slots + s] * block, -block)
         want = jnp.where(entry // block == s, live + entry % block, want)
     order = jnp.where(want == col_id, 1.0 / (wins * subs), 0.0).astype(jnp.bfloat16)
-
+    picks[...] = pick
+    orders[...] = order
+
+    for dp in range(pairs):
+        for d in range(subs - 1, -1, -1):
+            slot = (near[dp] * 2 + sec) * subs + lax.rem(sub + d, subs)
+            if dp or d:
+                send(slot, c_send.at[0, 0], {"section": 1 - sec}).wait_recv()
+            copies.append(send(slot, c_send.at[dp, d], {"section": 1 - sec}))
+            copies[-1].start()
+
+    for load in late:
+        load.wait()
     for dp in range(pairs):
         for d in range(subs):
             slot = (lax.rem(p + dp, pairs) * 2 + 1 - sec) * subs + lax.rem(sub + d, subs)
-            send(slot, z_send.at[0], {"section": 1 - sec}).wait_recv()
+            send(slot, c_send.at[0, 0], {"section": 1 - sec}).wait_recv()
 
     width = 2 * LANES
     wanted = slots * block
     edge = jnp.where(lax.broadcasted_iota(jnp.int32, (wanted, LANES), 1) == 0, 0.5, 1.0)
+    flats = [held[:, :, base * LANES : (base + 2) * LANES].reshape(depth, width) for base in range(0, RADIX, 2)]
+    heads = [jnp.dot(picks[...], flat, preferred_element_type=jnp.float32).astype(jnp.bfloat16) for flat in flats]
     for base in range(0, RADIX, 2):
-        flat = held[:, :, base * LANES : (base + 2) * LANES].reshape(depth, width)
-        heads = jnp.dot(pick, flat, preferred_element_type=jnp.float32).astype(jnp.bfloat16)
         for a in range(leads):
             for part in range(2):
                 at = (part * leads + a) * group
-                full = jnp.concatenate([heads[at : at + group, :]] * (pairs * 2), axis=0)
-                got = jnp.dot(order, flat * full, preferred_element_type=jnp.float32)
+                full = jnp.concatenate([heads[base // 2][at : at + group, :]] * (pairs * 2), axis=0)
+                got = jnp.dot(orders[...], flats[base // 2] * full, preferred_element_type=jnp.float32)
                 for h in range(2):
                     x = got[:, h * LANES : (h + 1) * LANES]
                     if base + h == 0:
                         x = x * edge
                     lhs[base + h, a * wanted : (a + 1) * wanted, part * LANES : (part + 1) * LANES] = x.astype(jnp.bfloat16)
-
-    for load in late:
-        load.wait()
 
     for h in range(2):
         for a in range(leads):
@@ -342,11 +338,12 @@
                 pltpu.VMEM((units, 2 * unit, NF // 2), jnp.bfloat16),
                 pltpu.VMEM((8, LANES), jnp.float32),
                 pltpu.VMEM((2 * LANES, LANES), jnp.float32),
+                pltpu.VMEM((4 * leads * subs * unit, 2 * units * unit), jnp.bfloat16),
+                pltpu.VMEM((slots * block, 2 * units * unit), jnp.bfloat16),
                 pltpu.VMEM((RADIX, total, 2 * LANES), jnp.bfloat16),
                 pltpu.VMEM(inverse.shape, jnp.bfloat16),
                 pltpu.VMEM(back.shape, jnp.float32),
                 pltpu.SemaphoreType.DMA((2,)),
-                pltpu.SemaphoreType.DMA((pairs,)),
                 pltpu.SemaphoreType.DMA((pairs, subs)),
                 pltpu.SemaphoreType.DMA((pairs, subs)),
                 pltpu.SemaphoreType.DMA((units,)),

time: 15.6 us -> 14.9 us (0.955)
  Pallas kernels: 14.7 us -> 14 us
    pallas_call x1, Pallas kernels: 14.7 us -> 14 us  [body(): pl.pallas_call(functools.partial(kernel, (pairs, subs, rows, wins, slots,...]
where the time goes in v2:
time: 14.9 us; the launch traced here: 14.8 us
  Pallas kernels  14 us (94%)
  local copies, waits for them, and re-layouts  0.8 us (5%)
    pallas_call x1, Pallas kernels, body(): pl.pallas_call(functools.partial(kernel, (pairs, subs, rows, wins, slots,...  14 us
    unnamed x1, local copies, waits for them, and re-layouts  0.8 us

profile of v2, /device:TPU:1, one launch (start us, length us, event | category | flops | bytes accessed | tf_op | source)
XLA Modules:
  0.0 14.8 jit_solution(124308956678846560)
XLA Ops:
  0.0 14.0 %shard_map.91 = f32[64,2048]{1,0:T(8,128)S(1)} custom-call(bf16[4,24576]{1,0:T(4,128)(2,1)} %raw_in.1, f32[1,64]{1,0:T(1,128)} %bitcast.5, s32[32]{0:T(128)} %ids_in.1, s32[2]{0:T(128)} %offs_in.1, s32[2,16]{1,0:T(2,128)} %bitcast.4, bf16[512,256]{1,0:T(8,128)(2,1)} %constant.8.clone.forward_in, f32[8,2,8,128]{3,2,1,0:T(8,128)} %constant.9.clone.twiddle_in, ...), custom_call_target="tpu_custom_call" | custom-call | tf_op jit(solution)/shard_map/pallas_call | solution.py:324
  14.0 0.8 %copy.11 = f32[2,4,8,2048]{3,2,1,0:T(8,128)} copy(f32[2,4,8,2048]{3,2,1,0:T(8,128)S(1)} %bitcast.3) | data formatting | bytes 1048576

commit v3 on v2

--- a/solution.py
+++ b/solution.py
@@ -80,22 +80,13 @@
 
 def kernel(sizes, raw_in, taps_in, ids_in, offs_in, table_in, forward_in, twiddle_in, inverse_in, back_in, out,
            raw, taps, ids, offs, table, forward, twiddle, in_sems,
-           held, tapf, shifted, picks, orders, lhs, inv, back, late_sems, x_send, c_send, recv):
+           held, tapf, shifted, picks, orders, lhs, inv, back, late_sems, x_send, c_send, swap, recv):
     pairs, subs, rows, wins, slots, leads = sizes
     unit = rows * wins
     block = 2 * rows
     p = lax.axis_index("pairs")
     sec = lax.axis_index("section")
     sub = lax.axis_index("sub")
-
-    barrier = pltpu.get_barrier_semaphore()
-    for dp in range(pairs):
-        for d in range(subs):
-            if dp or d:
-                pl.semaphore_signal(
-                    barrier, inc=1, device_id_type=MESH,
-                    device_id={"pairs": lax.rem(p + dp, pairs), "sub": lax.rem(sub + d, subs)})
-    pl.semaphore_signal(barrier, inc=1, device_id={"section": 1 - sec}, device_id_type=MESH)
 
     loads = [
         pltpu.make_async_copy(source, target, in_sems.at[i])
@@ -111,6 +102,15 @@
     ]
     for load in late:
         load.start()
+    barrier = pltpu.get_barrier_semaphore()
+    for dp in range(pairs):
+        for d in range(subs):
+            if dp or d:
+                pl.semaphore_signal(
+                    barrier, inc=1, device_id_type=MESH,
+                    device_id={"pairs": lax.rem(p + dp, pairs), "sub": lax.rem(sub + d, subs)})
+    pl.semaphore_signal(barrier, inc=1, device_id={"section": 1 - sec}, device_id_type=MESH)
+
     tapf[...] = jnp.zeros_like(tapf)
     span = raw_in.shape[1]
     raw[:, span:] = jnp.zeros((rows, raw.shape[1] - span), raw.dtype)
@@ -199,10 +199,10 @@
 
     pl.semaphore_wait(barrier, pairs * subs)
 
-    def send(slot, send_sem, device):
+    def send(slot, send_sem, device, arrival):
         return pltpu.make_async_remote_copy(
             src_ref=held.at[slot], dst_ref=held.at[slot], send_sem=send_sem,
-            recv_sem=recv.at[slot], device_id=device, device_id_type=MESH)
+            recv_sem=arrival, device_id=device, device_id_type=MESH)
 
     near = [p]
     for i in range(1, pairs):
@@ -210,13 +210,12 @@
         for q in range(pairs):
             at = jnp.where(p == q, sorted(range(pairs), key=lambda t: (abs(t - q), t))[i], at)
         near.append(at)
-    copies = []
+    here = p * subs + sub
     for dp in range(pairs - 1, -1, -1):
         for d in range(subs - 1, -1, -1):
-            if not (dp or d):
-                continue
-            copies.append(send(mine, x_send.at[dp, d], {"pairs": near[dp], "sub": lax.rem(sub + d, subs)}))
-            copies[-1].start()
+            if dp or d:
+                send(mine, x_send, {"pairs": near[dp], "sub": lax.rem(sub + d, subs)}, recv.at[here]).start()
+
     count = pairs * block
     tall = 2 * unit
     depth = pairs * 2 * subs * tall
@@ -249,18 +248,16 @@
 
     for dp in range(pairs):
         for d in range(subs - 1, -1, -1):
-            slot = (near[dp] * 2 + sec) * subs + lax.rem(sub + d, subs)
+            across = lax.rem(sub + d, subs)
+            slot = (near[dp] * 2 + sec) * subs + across
             if dp or d:
-                send(slot, c_send.at[0, 0], {"section": 1 - sec}).wait_recv()
-            copies.append(send(slot, c_send.at[dp, d], {"section": 1 - sec}))
-            copies[-1].start()
+                send(slot, x_send, {"section": 1 - sec}, recv.at[near[dp] * subs + across]).wait_recv()
+            send(slot, c_send, {"section": 1 - sec}, swap).start()
 
     for load in late:
         load.wait()
-    for dp in range(pairs):
-        for d in range(subs):
-            slot = (lax.rem(p + dp, pairs) * 2 + 1 - sec) * subs + lax.rem(sub + d, subs)
-            send(slot, c_send.at[0, 0], {"section": 1 - sec}).wait_recv()
+    half = pairs * subs
+    send(pl.ds(0, half), c_send, {"section": 1 - sec}, swap).wait_recv()
 
     width = 2 * LANES
     wanted = slots * block
@@ -301,8 +298,8 @@
                     column = (j + RADIX // 2) % RADIX * width + h * LANES
                     out[a * wanted + g * 8 : a * wanted + g * 8 + 8, column : column + LANES] = lags[j]
 
-    for copy in copies:
-        copy.wait_send()
+    send(pl.ds(0, half - 1), x_send, {"section": 1 - sec}, swap).wait_send()
+    send(pl.ds(0, half), c_send, {"section": 1 - sec}, swap).wait_send()
 
 
 def solution(mesh):
@@ -344,9 +341,10 @@
                 pltpu.VMEM(inverse.shape, jnp.bfloat16),
                 pltpu.VMEM(back.shape, jnp.float32),
                 pltpu.SemaphoreType.DMA((2,)),
-                pltpu.SemaphoreType.DMA((pairs, subs)),
-                pltpu.SemaphoreType.DMA((pairs, subs)),
-                pltpu.SemaphoreType.DMA((units,)),
+                pltpu.SemaphoreType.DMA,
+                pltpu.SemaphoreType.DMA,
+                pltpu.SemaphoreType.DMA,
+                pltpu.SemaphoreType.DMA((pairs * subs,)),
             ],
             compiler_params=pltpu.CompilerParams(
                 collective_id=0, has_side_effects=True, vmem_limit_bytes=48*2**20),

time: 14.9 us -> 14.8 us (level)
  Pallas kernels: 14 us -> 13.8 us
    pallas_call x1, Pallas kernels: 14 us -> 13.8 us  [body(): pl.pallas_call(functools.partial(kernel, (pairs, subs, rows, wins, slots,...]
where the time goes in v3:
time: 14.8 us; the launch traced here: 14.6 us
  Pallas kernels  13.8 us (93%)
  local copies, waits for them, and re-layouts  0.8 us (5%)
    pallas_call x1, Pallas kernels, body(): pl.pallas_call(functools.partial(kernel, (pairs, subs, rows, wins, slots,...  13.8 us
    unnamed x1, local copies, waits for them, and re-layouts  0.8 us

profile of v3, /device:TPU:1, one launch (start us, length us, event | category | flops | bytes accessed | tf_op | source)
XLA Modules:
  0.0 14.6 jit_solution(3762367849871777953)
XLA Ops:
  0.0 13.8 %shard_map.91 = f32[64,2048]{1,0:T(8,128)S(1)} custom-call(bf16[4,24576]{1,0:T(4,128)(2,1)} %raw_in.1, f32[1,64]{1,0:T(1,128)} %bitcast.5, s32[32]{0:T(128)} %ids_in.1, s32[2]{0:T(128)} %offs_in.1, s32[2,16]{1,0:T(2,128)} %bitcast.4, bf16[512,256]{1,0:T(8,128)(2,1)} %constant.8.clone.forward_in, f32[8,2,8,128]{3,2,1,0:T(8,128)} %constant.9.clone.twiddle_in, ...), custom_call_target="tpu_custom_call" | custom-call | tf_op jit(solution)/shard_map/pallas_call | solution.py:321
  13.8 0.8 %copy.11 = f32[2,4,8,2048]{3,2,1,0:T(8,128)} copy(f32[2,4,8,2048]{3,2,1,0:T(8,128)S(1)} %bitcast.3) | data formatting | bytes 1048576
